TPU v7x, 128 devices: a whole 4x4x4 slice. The times are simulated.
128 devices in a mesh: row: 16 (over z, y), proto: 8 (over x, core).
Axes of the slice: x: 4, y: 4, z: 4, core: 2. Of those that a mesh axis runs over, the one named last changes fastest.
Arguments:
- embeddings: bfloat16 [4096, 256], P('row')
- queue_feats: bfloat16 [8192, 256], P('row')
- prototypes: bfloat16 [256, 65536], P('row', 'proto')
- crop_image: int32 [4096], P('row'), may hold values from 0 to 511, as said below
- fill_count: int32 [1], replicated, may hold values from 4096 to 8192
Outputs:
- grad_embed: float32 [4096, 256], P('row')
- grad_proto: float32 [256, 65536], P('row', 'proto')
- loss: float32 [1], replicated
Inputs may be any that keep to these rules, and one draw needn't show every extreme that they name: `crop_image`: each image index is named by exactly 8 crops, all within one aligned block of 256 rows (the rows of one device); block b holds images b * 32 to (b + 1) * 32 - 1.
All inputs are finite; a program needn't handle non-finite values.
Results may differ from a plain program's by a relative error of at most 0.002.
Values may be sent and summed in bfloat16 or wider, within the bound.
A program may use at most 64 MiB of HBM per device.

v0:
```python
import jax
import jax.numpy as jnp
from jax import lax
from jax.sharding import PartitionSpec as P

CROPS = 8
ITERS = 3
ENTROPY_SMOOTHER = 0.05
SOFTMAX_TEMPER = 0.1


def unit_rows(raw):
    values = raw.astype(jnp.float32)
    inverse = lax.rsqrt(jnp.sum(values * values, axis=1, keepdims=True) + 1e-06)
    return (values * inverse, inverse)


def body(embeddings, queue_feats, prototypes, crop_image, fill_count):
    normed_exact, inverse = unit_rows(embeddings)
    normed = normed_exact.astype(jnp.bfloat16)
    queue_normed = unit_rows(queue_feats)[0].astype(jnp.bfloat16)
    batch_rows = normed.shape[0]
    queue_rows = queue_normed.shape[0]
    feat_dim = normed.shape[1]
    image_local = batch_rows // CROPS
    local_image = crop_image - lax.axis_index("row") * image_local
    image_ids = jnp.arange(image_local, dtype=jnp.int32)
    membership = (image_ids[:, None] == local_image[None, :]).astype(jnp.bfloat16)
    gathered = lax.all_gather(prototypes, "row", axis=0, tiled=True)
    width_local = gathered.shape[1]
    block_cols = min(512, width_local)
    block_count = width_local // block_cols
    blocks = gathered.reshape(feat_dim, block_count, block_cols).transpose(1, 0, 2)
    offset = lax.axis_index("row") * queue_rows
    queue_live = (offset + jnp.arange(queue_rows, dtype=jnp.int32) < fill_count[0]).astype(
        jnp.float32
    )
    live = jnp.concatenate([jnp.ones((batch_rows,), jnp.float32), queue_live])
    rows_all = jnp.concatenate([normed, queue_normed], axis=0)

    def row_pass(column):

        def row_block(cumulative_accumulator, inputs_pair):
            proto_block, cluster_rescaling = inputs_pair
            centroid_similarity = jnp.dot(rows_all, proto_block, preferred_element_type=jnp.float32)
            return (
                cumulative_accumulator
                + jnp.sum(
                    jnp.exp(centroid_similarity / ENTROPY_SMOOTHER) * cluster_rescaling[None, :],
                    axis=1,
                ),
                None,
            )

        row_total, _ = lax.scan(
            row_block,
            jnp.zeros((rows_all.shape[0],), jnp.float32),
            (blocks, column.reshape(block_count, block_cols)),
        )
        return row_total

    centroid_matrix = live
    column = jnp.zeros((width_local,), jnp.float32)
    for sweep_index in range(ITERS):

        def column_block(proto_block):
            centroid_similarity = jnp.dot(rows_all, proto_block, preferred_element_type=jnp.float32)
            return jnp.sum(
                jnp.exp(centroid_similarity / ENTROPY_SMOOTHER) * centroid_matrix[:, None], axis=0
            )

        column = 1.0 / lax.psum(lax.map(column_block, blocks).reshape(width_local), "row")
        if sweep_index + 1 < ITERS:
            centroid_matrix = live / lax.psum(row_pass(column), "proto")
    column_blocks = column.reshape(block_count, block_cols)

    def totals(cumulative_accumulator, inputs_pair):
        proto_block, cluster_rescaling = inputs_pair
        centroid_similarity = jnp.dot(normed, proto_block, preferred_element_type=jnp.float32)
        allotment_share = jnp.sum(
            jnp.exp(centroid_similarity / ENTROPY_SMOOTHER) * cluster_rescaling[None, :], axis=1
        )
        softmax_portion = jnp.sum(jnp.exp(centroid_similarity / SOFTMAX_TEMPER), axis=1)
        return (
            (
                cumulative_accumulator[0] + allotment_share,
                cumulative_accumulator[1] + softmax_portion,
            ),
            None,
        )

    zeros_batch = jnp.zeros((batch_rows,), jnp.float32)
    (code_local, soft_local), _ = lax.scan(
        totals, (zeros_batch, zeros_batch), (blocks, column_blocks)
    )
    overall_mass_sum, softmax_total = lax.psum((code_local, soft_local), "proto")
    log_grand_total = jnp.log(softmax_total)
    member_weights = membership.astype(jnp.float32)

    def slopes(cumulative_accumulator, inputs_pair):
        proto_block, cluster_rescaling = inputs_pair
        centroid_similarity = jnp.dot(normed, proto_block, preferred_element_type=jnp.float32)
        cluster_allotment = (
            jnp.exp(centroid_similarity / ENTROPY_SMOOTHER)
            * cluster_rescaling[None, :]
            / overall_mass_sum[:, None]
        )
        per_image = jnp.dot(member_weights, cluster_allotment, precision=lax.Precision.HIGHEST)
        grouped = lax.dot_general(
            member_weights, per_image, (((0,), (0,)), ((), ())), precision=lax.Precision.HIGHEST
        )
        target_codes = (grouped - cluster_allotment) / (CROPS - 1)
        predicted_probs = jnp.exp(centroid_similarity / SOFTMAX_TEMPER) / softmax_total[:, None]
        logit_gradient = ((predicted_probs - target_codes) / SOFTMAX_TEMPER).astype(jnp.bfloat16)
        loss_portion = jnp.sum(
            target_codes * (log_grand_total[:, None] - centroid_similarity / SOFTMAX_TEMPER)
        )
        return (cumulative_accumulator + loss_portion, logit_gradient)

    loss_local, grad_blocks = lax.scan(slopes, jnp.zeros((), jnp.float32), (blocks, column_blocks))
    logit_gradient = grad_blocks.transpose(1, 0, 2).reshape(batch_rows, width_local)
    normed_local = lax.dot_general(
        logit_gradient, gathered, (((1,), (1,)), ((), ())), preferred_element_type=jnp.float32
    )
    normed_grad = lax.psum(normed_local, "proto")
    grad_proto = lax.psum_scatter(
        lax.dot_general(
            normed, logit_gradient, (((0,), (0,)), ((), ())), preferred_element_type=jnp.float32
        ),
        "row",
        scatter_dimension=0,
        tiled=True,
    )
    loss_total = lax.psum(loss_local, ("row", "proto"))
    loss = loss_total / (batch_rows * lax.axis_size("row"))
    grad_embed = inverse * (
        normed_grad - normed_exact * jnp.sum(normed_exact * normed_grad, axis=1, keepdims=True)
    )
    return (grad_embed, grad_proto, loss.reshape(1))


def solution(mesh):
    placed = (P("row", None), P("row", None), P("row", "proto"), P("row"), P())
    return jax.shard_map(
        body,
        mesh=mesh,
        in_specs=placed,
        out_specs=(P("row", None), P("row", "proto"), P()),
        check_vma=False,
    )
```

profile of v0, /device:TPU:0, one launch (start us, length us, event | category | flops | bytes accessed | tf_op | source)
XLA Modules:
  0.0 706.2 jit_solution(11963652205974593261)
XLA Ops:
  13.7 50.5 %all-gather.2.cloned.1.call-done = bf16[256,8192]{1,0:T(8,128)(2,1)} async-done(((bf16[16,8192]{1,0:T(8,128)(2,1)}), bf16[256,8192]{1,0:T(8,128)(2,1)}) %all-gather.2.cloned.1.call-update) | async-done | bytes 4194320 | tf_op jit(solution)/shard_map/all_gather | solution.py:29
  64.2 6.4 copy.16
  70.5 6.4 copy.23
  77.0 25.4 %while.78 = (s32[]{:T(128)}, f32[16,512]{1,0:T(8,128)S(1)}, bf16[16,256,512]{2,1,0:T(8,128)(2,1)}, bf16[768,256]{1,0:T(8,128)(2,1)S(1)}, f32[768]{0:T(1024)S(1)}, /*index=5*/s32[]{:T(128)}, s32[]{:T(128)}) while((s32[]{:T(128)}, f32[16,512]{1,0:T(8,128)S(1)}, bf16[16,256,512]{2,1,0:T(8,128)(2,1)}, bf16[768,256]{1,0:T(8,128)(2,1)S(1)}, ...), condition=%wide.region_4.5_spmd, body=%wide.region_2.4_spmd.sunk | while | flops 202505728 | bytes 664669 | solution.py:72
  81.7 1.5 multiply_reduce_fusion.13
  86.5 1.5 multiply_reduce_fusion.13
  91.3 1.5 multiply_reduce_fusion.13
  96.1 1.5 multiply_reduce_fusion.13
  100.8 1.5 multiply_reduce_fusion.13
  102.4 72.4 %psum.63 = f32[8192]{0:T(1024)S(1)} all-reduce(f32[8192]{0:T(1024)S(1)} %bitcast.113), channel_id=1, replica_groups=mesh['row'=16,'proto'=8] {'row'}, use_global_device_ids=true, to_apply=%region_5.6 | all-reduce | flops 8192 | bytes 65536 | tf_op jit(solution)/shard_map/psum | solution.py:72
  174.9 24.7 %while.82 = (s32[]{:T(128)}, f32[768]{0:T(1024)S(1)}, bf16[16,256,512]{2,1,0:T(8,128)(2,1)}, bf16[768,256]{1,0:T(8,128)(2,1)S(1)}, f32[16,512]{1,0:T(8,128)S(1)}, /*index=5*/s32[]{:T(128)}, s32[]{:T(128)}) while((s32[]{:T(128)}, f32[768]{0:T(1024)S(1)}, bf16[16,256,512]{2,1,0:T(8,128)(2,1)}, bf16[768,256]{1,0:T(8,128)(2,1)S(1)}, ...), condition=%wide.region_8.9_spmd.clone, body=%wide.region_6.8_spmd.clone.sunk | while | flops 202507008 | bytes 673895 | solution.py:55
  199.6 12.4 %psum.64 = f32[768]{0:T(1024)S(1)} all-reduce(f32[768]{0:T(1024)S(1)} %get-tuple-element.225), channel_id=1, replica_groups=mesh['row'=16,'proto'=8] {'proto'}, use_global_device_ids=true, to_apply=%region_9.10 | all-reduce | flops 768 | bytes 6144 | tf_op jit(solution)/shard_map/psum | solution.py:74
  212.0 25.5 %while.79 = (s32[]{:T(128)}, f32[16,512]{1,0:T(8,128)S(1)}, bf16[16,256,512]{2,1,0:T(8,128)(2,1)}, bf16[768,256]{1,0:T(8,128)(2,1)S(1)}, f32[768]{0:T(1024)S(1)}, /*index=5*/s32[]{:T(128)}, s32[]{:T(128)}) while((s32[]{:T(128)}, f32[16,512]{1,0:T(8,128)S(1)}, bf16[16,256,512]{2,1,0:T(8,128)(2,1)}, bf16[768,256]{1,0:T(8,128)(2,1)S(1)}, ...), condition=%wide.region_12.13_spmd, body=%wide.region_10.12_spmd.sunk | while | flops 202505728 | bytes 664669 | solution.py:72
  215.2 1.5 multiply_reduce_fusion.14
  220.0 1.5 multiply_reduce_fusion.14
  224.7 1.5 multiply_reduce_fusion.14
  229.5 1.5 multiply_reduce_fusion.14
  234.3 1.5 multiply_reduce_fusion.14
  237.5 69.5 %psum.65 = f32[8192]{0:T(1024)S(1)} all-reduce(f32[8192]{0:T(1024)S(1)} %bitcast.114), channel_id=1, replica_groups=mesh['row'=16,'proto'=8] {'row'}, use_global_device_ids=true, to_apply=%region_13.14 | all-reduce | flops 8192 | bytes 65536 | tf_op jit(solution)/shard_map/psum | solution.py:72
  307.1 24.7 %while.83 = (s32[]{:T(128)}, f32[768]{0:T(1024)S(1)}, bf16[16,256,512]{2,1,0:T(8,128)(2,1)}, bf16[768,256]{1,0:T(8,128)(2,1)S(1)}, f32[16,512]{1,0:T(8,128)S(1)}, /*index=5*/s32[]{:T(128)}, s32[]{:T(128)}) while((s32[]{:T(128)}, f32[768]{0:T(1024)S(1)}, bf16[16,256,512]{2,1,0:T(8,128)(2,1)}, bf16[768,256]{1,0:T(8,128)(2,1)S(1)}, ...), condition=%wide.region_16.17_spmd.clone, body=%wide.region_14.16_spmd.clone.sunk | while | flops 202507008 | bytes 673895 | solution.py:55
  331.7 12.4 %psum.66 = f32[768]{0:T(1024)S(1)} all-reduce(f32[768]{0:T(1024)S(1)} %get-tuple-element.227), channel_id=1, replica_groups=mesh['row'=16,'proto'=8] {'proto'}, use_global_device_ids=true, to_apply=%region_17.18 | all-reduce | flops 768 | bytes 6144 | tf_op jit(solution)/shard_map/psum | solution.py:74
  344.2 25.5 %while.80 = (s32[]{:T(128)}, f32[16,512]{1,0:T(8,128)S(1)}, bf16[16,256,512]{2,1,0:T(8,128)(2,1)}, bf16[768,256]{1,0:T(8,128)(2,1)S(1)}, f32[768]{0:T(1024)S(1)}, /*index=5*/s32[]{:T(128)}, s32[]{:T(128)}) while((s32[]{:T(128)}, f32[16,512]{1,0:T(8,128)S(1)}, bf16[16,256,512]{2,1,0:T(8,128)(2,1)}, bf16[768,256]{1,0:T(8,128)(2,1)S(1)}, ...), condition=%wide.region_20.21_spmd, body=%wide.region_18.20_spmd.sunk | while | flops 202505728 | bytes 664669 | solution.py:72
  347.4 1.5 multiply_reduce_fusion.15
  369.7 69.5 %psum.67 = f32[8192]{0:T(1024)S(1)} all-reduce(f32[8192]{0:T(1024)S(1)} %bitcast.115), channel_id=1, replica_groups=mesh['row'=16,'proto'=8] {'row'}, use_global_device_ids=true, to_apply=%region_21.22 | all-reduce | flops 8192 | bytes 65536 | tf_op jit(solution)/shard_map/psum | solution.py:72
  439.2 22.2 %while.84 = (s32[]{:T(128)}, f32[256]{0:T(256)S(1)}, f32[256]{0:T(256)S(1)}, bf16[16,256,512]{2,1,0:T(8,128)(2,1)}, bf16[256,256]{1,0:T(8,128)(2,1)S(1)}, /*index=5*/f32[16,512]{1,0:T(8,128)S(1)}, s32[]{:T(128)}, s32[]{:T(128)}) while((s32[]{:T(128)}, f32[256]{0:T(256)S(1)}, f32[256]{0:T(256)S(1)}, ...), condition=%wide.region_25.26_spmd.clone, body=%wide.region_22.25_spmd.clone.sunk | while | flops 67764736 | bytes 407663 | solution.py:93
  461.4 12.4 %all-reduce.1 = (f32[256]{0:T(256)S(1)}, f32[256]{0:T(256)S(1)}) all-reduce(f32[256]{0:T(256)S(1)} %get-tuple-element.229, f32[256]{0:T(256)S(1)} %get-tuple-element.230), channel_id=1, replica_groups=mesh['row'=16,'proto'=8] {'proto'}, use_global_device_ids=true, to_apply=%region_26.27 | all-reduce | flops 512 | bytes 4096 | tf_op jit(solution)/shard_map/psum | solution.py:96
  473.8 76.1 %while.81 = (s32[]{:T(128)}, f32[]{:T(128)}, bf16[16,256,512]{1,2,0:T(8,128)(2,1)}, bf16[16,256,512]{2,1,0:T(8,128)(2,1)}, bf16[256,256]{1,0:T(8,128)(2,1)S(1)},...) while((s32[]{:T(128)}, f32[]{:T(128)}, ...), condition=%wide.region_30.31_spmd.clone, body=%wide.region_28.30_spmd.clone.sunk | while | flops 170049536 | bytes 3946641 | solution.py:120
  550.0 5.5 fusion.45
  555.5 6.7 fusion.46
  562.3 62.9 %psum.71 = f32[]{:T(128)} all-reduce(f32[]{:T(128)} %get-tuple-element.232), channel_id=1, replica_groups=mesh['row'=16,'proto'=8] {'row','proto'}, use_global_device_ids=true, to_apply=%region_34.35 | all-reduce | flops 1 | bytes 8 | tf_op jit(solution)/shard_map/psum | solution.py:134
  627.0 1.8 fusion.41
  628.8 69.7 %reduce-scatter.2.cloned.1.call-done = f32[16,8192]{1,0:T(8,128)} async-done(((f32[256,8192]{1,0:T(8,128)}), f32[16,8192]{1,0:T(8,128)}) %reduce-scatter.2.cloned.1.call-update) | async-done | bytes 524304 | tf_op jit(solution)/shard_map/reduce_scatter | solution.py:126
  (349 shorter events, 200.9 us)
Async XLA Ops:
  7.2 57.0 %all-gather.2.cloned.1.call-start = ((), (), s32[]{:S(2)}) async-start(), calls=%async_computation.1 | async-start | bytes 4456448 | tf_op jit(solution)/shard_map/all_gather | solution.py:29
  7.9 617.9 %all-reduce.4.cloned.1.call-start = ((), (), s32[]{:S(2)}) async-start(), calls=%async_computation.2 | async-start | bytes 524288 | tf_op jit(solution)/shard_map/psum | solution.py:125
  555.5 143.1 %reduce-scatter.2.cloned.1.call-start = ((), (), s32[]{:S(2)}) async-start(), calls=%async_computation.3 | async-start | bytes 8912896 | tf_op jit(solution)/shard_map/reduce_scatter | solution.py:126
  562.2 63.6 %copy-start = (bf16[256,256]{1,0:T(8,128)(2,1)S(1)}, bf16[256,256]{1,0:T(8,128)(2,1)}, u32[]{:S(2)}) copy-start(bf16[256,256]{1,0:T(8,128)(2,1)} %param.19) | copy-start | bytes 393220
Sparse Core Ops, SparseCore 0:
  10.1 53.9 all-gather.1
  555.6 53.6 all-reduce.3
  613.2 85.2 reduce-scatter.1
where the time goes:
time: 711 us; the launch traced here: 706 us
  blocking collectives  312 us (44%)
  matrix products  205 us (29%)
  waiting for transfers between devices  121 us (17%)
  other arithmetic  21.7 us (3%)
  local copies, waits for them, and re-layouts  16.4 us (2%)
  between operations  16.4 us (2%)
  loops' own time  13.6 us (2%)
    psum x3, blocking collectives, body(): lax.psum(lax.map(column_block, blocks).reshape(width_local), 'row')  212 us
    dot_general x48, matrix products, column_block(): jnp.dot(rows_all, proto_block, preferred_element_type=jnp.float32)  72.5 us
    reduce_scatter x1, waiting for transfers between devices, body(): lax.psum_scatter(lax.dot_general(normed, logit_gradient, (((0,), (0,)), (...  69.7 us
    psum x1, blocking collectives, body(): loss_total = lax.psum(loss_local, ('row', 'proto'))  62.9 us
    all_gather x1, waiting for transfers between devices, body(): gathered = lax.all_gather(prototypes, 'row', axis=0, tiled=True)  50.5 us
    dot_general x32, matrix products, row_block(): jnp.dot(rows_all, proto_block, preferred_element_type=jnp.float32)  47.4 us
    psum x2, blocking collectives, body(): centroid_matrix = live / lax.psum(row_pass(column), 'proto')  24.9 us
    dot_general x16, matrix products, totals(): jnp.dot(normed, proto_block, preferred_element_type=jnp.float32)  21.2 us
  transfers between devices with their start and end apart: 3, of which 2 were waited for; matrix products, arithmetic and copies ran while one was open for 2% of the time, Pallas kernels for 0%

commit v1 on v0

--- a/solution.py
+++ b/solution.py
@@ -26,7 +26,10 @@
     local_image = crop_image - lax.axis_index("row") * image_local
     image_ids = jnp.arange(image_local, dtype=jnp.int32)
     membership = (image_ids[:, None] == local_image[None, :]).astype(jnp.bfloat16)
-    gathered = lax.all_gather(prototypes, "row", axis=0, tiled=True)
+    peers = lax.axis_size("row")
+    parts = jnp.stack([prototypes for _ in range(peers)])
+    parts = lax.all_to_all(parts, "row", split_axis=0, concat_axis=0)
+    gathered = jnp.concatenate(parts, axis=0)
     width_local = gathered.shape[1]
     block_cols = min(512, width_local)
     block_count = width_local // block_cols

time: 711 us -> 665 us (0.935)
  waiting for transfers between devices: 121 us -> 73.8 us
  starting transfers between devices: 0.12 us -> 8.43 us
    all_to_all x0 -> x1, waiting for transfers between devices: none -> 61.9 us  [body(): parts = lax.all_to_all(parts, 'row', split_axis=0, concat_axis=0)]
    reduce_scatter x1, waiting for transfers between devices: 69.7 us -> 11.8 us  [body(): lax.psum_scatter(lax.dot_general(normed, logit_gradient, (((0,), (0,)), (...]
    all_gather x1 -> x0, waiting for transfers between devices: 50.5 us -> none  [body(): gathered = lax.all_gather(prototypes, 'row', axis=0, tiled=True)]
    all_to_all x0 -> x1, starting transfers between devices: none -> 8.34 us  [body(): parts = lax.all_to_all(parts, 'row', split_axis=0, concat_axis=0)]
where the time goes in v1:
time: 665 us; the launch traced here: 661 us
  blocking collectives  312 us (47%)
  matrix products  202 us (30%)
  waiting for transfers between devices  73.8 us (11%)
  between operations  18.2 us (3%)
  other arithmetic  17.3 us (3%)
  local copies, waits for them, and re-layouts  15.3 us (2%)
  loops' own time  13.6 us (2%)
  starting transfers between devices  8.43 us (1%)
    psum x3, blocking collectives, body(): lax.psum(lax.map(column_block, blocks).reshape(width_local), 'row')  211 us
    dot_general x48, matrix products, column_block(): jnp.dot(rows_all, proto_block, preferred_element_type=jnp.float32)  72.5 us
    psum x1, blocking collectives, body(): loss_total = lax.psum(loss_local, ('row', 'proto'))  64.2 us
    all_to_all x1, waiting for transfers between devices, body(): parts = lax.all_to_all(parts, 'row', split_axis=0, concat_axis=0)  61.9 us
    dot_general x32, matrix products, row_block(): jnp.dot(rows_all, proto_block, preferred_element_type=jnp.float32)  47.4 us
    psum x2, blocking collectives, body(): centroid_matrix = live / lax.psum(row_pass(column), 'proto')  24.9 us
    dot_general x16, matrix products, totals(): jnp.dot(normed, proto_block, preferred_element_type=jnp.float32)  21.2 us
    dot_general x16, matrix products, slopes(): lax.dot_general(member_weights, per_image, (((0,), (0,)), ((), ())), prec...  19.5 us
  transfers between devices with their start and end apart: 3, of which 2 were waited for; matrix products, arithmetic and copies ran while one was open for 2% of the time, Pallas kernels for 0%

profile of v1, /device:TPU:0, one launch (start us, length us, event | category | flops | bytes accessed | tf_op | source)
XLA Modules:
  0.0 661.1 jit_solution(15858840810303205915)
XLA Ops:
  8.0 3.4 stack.2
  11.4 8.3 %all-to-all-start = ((bf16[16,16,8192]{2,1,0:T(8,128)(2,1)}), bf16[16,16,8192]{2,1,0:T(8,128)(2,1)}, u32[]{:S(2)}, u32[]{:S(2)}) async-start(bf16[16,16,8192]{2,1,0:T(8,128)(2,1)} %stack.2), calls=%async_computation | async-start | bytes 8388608 | tf_op jit(solution)/shard_map/all_to_all | solution.py:31
  21.1 61.9 %all-to-all-done = bf16[16,16,8192]{2,1,0:T(8,128)(2,1)} async-done(((bf16[16,16,8192]{2,1,0:T(8,128)(2,1)}), bf16[16,16,8192]{2,1,0:T(8,128)(2,1)}, u32[]{:S(2)}, u32[]{:S(2)}) %all-to-all-start) | async-done | bytes 4194336 | tf_op jit(solution)/shard_map/all_to_all | solution.py:31
  83.0 4.0 copy.15
  87.1 4.4 copy.14
  91.4 25.4 %while.78 = (s32[]{:T(128)}, f32[16,512]{1,0:T(8,128)S(1)}, bf16[16,256,512]{2,1,0:T(8,128)(2,1)}, bf16[768,256]{1,0:T(8,128)(2,1)S(1)}, f32[768]{0:T(1024)S(1)}, /*index=5*/s32[]{:T(128)}, s32[]{:T(128)}) while((s32[]{:T(128)}, f32[16,512]{1,0:T(8,128)S(1)}, bf16[16,256,512]{2,1,0:T(8,128)(2,1)}, bf16[768,256]{1,0:T(8,128)(2,1)S(1)}, ...), condition=%wide.region_4.5_spmd, body=%wide.region_2.4_spmd.sunk | while | flops 202505728 | bytes 664669 | solution.py:75
  93.0 1.5 multiply_reduce_fusion.13
  116.9 71.6 %psum.63 = f32[8192]{0:T(1024)S(1)} all-reduce(f32[8192]{0:T(1024)S(1)} %bitcast.116), channel_id=1, replica_groups=mesh['row'=16,'proto'=8] {'row'}, use_global_device_ids=true, to_apply=%region_5.6 | all-reduce | flops 8192 | bytes 65536 | tf_op jit(solution)/shard_map/psum | solution.py:75
  188.5 24.6 %while.82 = (s32[]{:T(128)}, f32[768]{0:T(1024)S(1)}, bf16[16,256,512]{2,1,0:T(8,128)(2,1)}, bf16[768,256]{1,0:T(8,128)(2,1)S(1)}, f32[16,512]{1,0:T(8,128)S(1)}, /*index=5*/s32[]{:T(128)}, s32[]{:T(128)}) while((s32[]{:T(128)}, f32[768]{0:T(1024)S(1)}, bf16[16,256,512]{2,1,0:T(8,128)(2,1)}, bf16[768,256]{1,0:T(8,128)(2,1)S(1)}, ...), condition=%wide.region_8.9_spmd.clone, body=%wide.region_6.8_spmd.clone.sunk | while | flops 202507008 | bytes 673895 | solution.py:58
  213.1 12.4 %psum.64 = f32[768]{0:T(1024)S(1)} all-reduce(f32[768]{0:T(1024)S(1)} %get-tuple-element.225), channel_id=1, replica_groups=mesh['row'=16,'proto'=8] {'proto'}, use_global_device_ids=true, to_apply=%region_9.10 | all-reduce | flops 768 | bytes 6144 | tf_op jit(solution)/shard_map/psum | solution.py:77
  225.5 25.5 %while.79 = (s32[]{:T(128)}, f32[16,512]{1,0:T(8,128)S(1)}, bf16[16,256,512]{2,1,0:T(8,128)(2,1)}, bf16[768,256]{1,0:T(8,128)(2,1)S(1)}, f32[768]{0:T(1024)S(1)}, /*index=5*/s32[]{:T(128)}, s32[]{:T(128)}) while((s32[]{:T(128)}, f32[16,512]{1,0:T(8,128)S(1)}, bf16[16,256,512]{2,1,0:T(8,128)(2,1)}, bf16[768,256]{1,0:T(8,128)(2,1)S(1)}, ...), condition=%wide.region_12.13_spmd, body=%wide.region_10.12_spmd.sunk | while | flops 202505728 | bytes 664669 | solution.py:75
  225.6 1.5 multiply_reduce_fusion.14
  227.2 1.5 multiply_reduce_fusion.14
  228.7 1.5 multiply_reduce_fusion.14
  251.0 69.5 %psum.65 = f32[8192]{0:T(1024)S(1)} all-reduce(f32[8192]{0:T(1024)S(1)} %bitcast.117), channel_id=1, replica_groups=mesh['row'=16,'proto'=8] {'row'}, use_global_device_ids=true, to_apply=%region_13.14 | all-reduce | flops 8192 | bytes 65536 | tf_op jit(solution)/shard_map/psum | solution.py:75
  320.6 24.7 %while.83 = (s32[]{:T(128)}, f32[768]{0:T(1024)S(1)}, bf16[16,256,512]{2,1,0:T(8,128)(2,1)}, bf16[768,256]{1,0:T(8,128)(2,1)S(1)}, f32[16,512]{1,0:T(8,128)S(1)}, /*index=5*/s32[]{:T(128)}, s32[]{:T(128)}) while((s32[]{:T(128)}, f32[768]{0:T(1024)S(1)}, bf16[16,256,512]{2,1,0:T(8,128)(2,1)}, bf16[768,256]{1,0:T(8,128)(2,1)S(1)}, ...), condition=%wide.region_16.17_spmd.clone, body=%wide.region_14.16_spmd.clone.sunk | while | flops 202507008 | bytes 673895 | solution.py:58
  345.3 12.4 %psum.66 = f32[768]{0:T(1024)S(1)} all-reduce(f32[768]{0:T(1024)S(1)} %get-tuple-element.227), channel_id=1, replica_groups=mesh['row'=16,'proto'=8] {'proto'}, use_global_device_ids=true, to_apply=%region_17.18 | all-reduce | flops 768 | bytes 6144 | tf_op jit(solution)/shard_map/psum | solution.py:77
  357.7 25.5 %while.80 = (s32[]{:T(128)}, f32[16,512]{1,0:T(8,128)S(1)}, bf16[16,256,512]{2,1,0:T(8,128)(2,1)}, bf16[768,256]{1,0:T(8,128)(2,1)S(1)}, f32[768]{0:T(1024)S(1)}, /*index=5*/s32[]{:T(128)}, s32[]{:T(128)}) while((s32[]{:T(128)}, f32[16,512]{1,0:T(8,128)S(1)}, bf16[16,256,512]{2,1,0:T(8,128)(2,1)}, bf16[768,256]{1,0:T(8,128)(2,1)S(1)}, ...), condition=%wide.region_20.21_spmd, body=%wide.region_18.20_spmd.sunk | while | flops 202505728 | bytes 664669 | solution.py:75
  360.9 1.5 multiply_reduce_fusion.15
  365.7 1.5 multiply_reduce_fusion.15
  370.5 1.5 multiply_reduce_fusion.15
  375.2 1.5 multiply_reduce_fusion.15
  380.0 1.5 multiply_reduce_fusion.15
  383.2 69.5 %psum.67 = f32[8192]{0:T(1024)S(1)} all-reduce(f32[8192]{0:T(1024)S(1)} %bitcast.118), channel_id=1, replica_groups=mesh['row'=16,'proto'=8] {'row'}, use_global_device_ids=true, to_apply=%region_21.22 | all-reduce | flops 8192 | bytes 65536 | tf_op jit(solution)/shard_map/psum | solution.py:75
  452.8 22.2 %while.84 = (s32[]{:T(128)}, f32[256]{0:T(256)S(1)}, f32[256]{0:T(256)S(1)}, bf16[16,256,512]{2,1,0:T(8,128)(2,1)}, bf16[256,256]{1,0:T(8,128)(2,1)S(1)}, /*index=5*/f32[16,512]{1,0:T(8,128)S(1)}, s32[]{:T(128)}, s32[]{:T(128)}) while((s32[]{:T(128)}, f32[256]{0:T(256)S(1)}, f32[256]{0:T(256)S(1)}, ...), condition=%wide.region_25.26_spmd.clone, body=%wide.region_22.25_spmd.clone.sunk | while | flops 67764736 | bytes 407663 | solution.py:96
  474.9 12.6 %all-reduce.1 = (f32[256]{0:T(256)S(1)}, f32[256]{0:T(256)S(1)}) all-reduce(f32[256]{0:T(256)S(1)} %get-tuple-element.229, f32[256]{0:T(256)S(1)} %get-tuple-element.230), channel_id=1, replica_groups=mesh['row'=16,'proto'=8] {'proto'}, use_global_device_ids=true, to_apply=%region_26.27 | all-reduce | flops 512 | bytes 4096 | tf_op jit(solution)/shard_map/psum | solution.py:99
  487.6 73.1 %while.81 = (s32[]{:T(128)}, f32[]{:T(128)}, bf16[16,256,512]{1,2,0:T(8,128)(2,1)}, bf16[16,256,512]{2,1,0:T(8,128)(2,1)}, bf16[256,256]{1,0:T(8,128)(2,1)S(1)},...) while((s32[]{:T(128)}, f32[]{:T(128)}, ...), condition=%wide.region_30.31_spmd.clone, body=%wide.region_28.30_spmd.clone.sunk | while | flops 170049536 | bytes 3946641 | solution.py:123
  560.6 5.5 fusion.45
  566.2 6.7 %fusion.46 = f32[256,8192]{1,0:T(8,128)} fusion(bf16[256,256]{1,0:T(8,128)(2,1)S(1)} %get-tuple-element.878, bf16[256,8192]{0,1:T(8,128)(2,1)} %bitcast.112), kind=kOutput, calls=%fused_computation.77 | convolution fusion | flops 1073741824 | bytes 12713984 | tf_op jit(solution)/shard_map/dot_general | solution.py:130
  572.9 64.2 %psum.71 = f32[]{:T(128)} all-reduce(f32[]{:T(128)} %get-tuple-element.232), channel_id=1, replica_groups=mesh['row'=16,'proto'=8] {'row','proto'}, use_global_device_ids=true, to_apply=%region_34.35 | all-reduce | flops 1 | bytes 8 | tf_op jit(solution)/shard_map/psum | solution.py:137
  638.9 1.8 fusion.41
  640.7 11.8 %reduce-scatter.2.cloned.1.call-done = f32[16,8192]{1,0:T(8,128)} async-done(((f32[256,8192]{1,0:T(8,128)}), f32[16,8192]{1,0:T(8,128)}) %reduce-scatter.2.cloned.1.call-update) | async-done | bytes 524304 | tf_op jit(solution)/shard_map/reduce_scatter | solution.py:129
  (353 shorter events, 195.7 us)
Async XLA Ops:
  11.4 9.1 %copy-start = (bf16[256,256]{1,0:T(8,128)(2,1)S(1)}, bf16[256,256]{1,0:T(8,128)(2,1)}, u32[]{:S(2)}) copy-start(bf16[256,256]{1,0:T(8,128)(2,1)} %param.19) | copy-start | bytes 393220
  11.4 9.3 %copy-start.1 = (bf16[512,256]{1,0:T(8,128)(2,1)S(1)}, bf16[512,256]{1,0:T(8,128)(2,1)}, u32[]{:S(2)}) copy-start(bf16[512,256]{1,0:T(8,128)(2,1)} %param.20) | copy-start | bytes 786436
  11.4 9.7 %copy-start.2 = (s32[256]{0:T(256)S(1)}, s32[256]{0:T(256)}, u32[]{:S(2)}) copy-start(s32[256]{0:T(256)} %param.22) | copy-start | bytes 3076
  11.4 71.6 %all-to-all-start = ((bf16[16,16,8192]{2,1,0:T(8,128)(2,1)}), bf16[16,16,8192]{2,1,0:T(8,128)(2,1)}, u32[]{:S(2)}, u32[]{:S(2)}) async-start(bf16[16,16,8192]{2,1,0:T(8,128)(2,1)} %stack.2), calls=%async_computation | async-start | bytes 8388608 | tf_op jit(solution)/shard_map/all_to_all | solution.py:31
  19.7 618.1 %all-reduce.4.cloned.1.call-start = ((), (), s32[]{:S(2)}) async-start(), calls=%async_computation.2 | async-start | bytes 524288 | tf_op jit(solution)/shard_map/psum | solution.py:128
  566.1 86.5 %reduce-scatter.2.cloned.1.call-start = ((), (), s32[]{:S(2)}) async-start(), calls=%async_computation.3 | async-start | bytes 8912896 | tf_op jit(solution)/shard_map/reduce_scatter | solution.py:129
Sparse Core Ops, SparseCore 0:
  566.2 54.1 all-reduce.3
Sparse Core Ops, SparseCore 1:
  573.0 79.5 reduce-scatter.1
